TPU v7x, 256 devices: a whole 4x4x8 slice. The times are simulated.
256 devices in a mesh: rep: 16 (over x, z_hi), tp: 16 (over y, z_lo, core).
Axes of the slice: x: 4, y: 4, z: 8 (z_hi: 4, z_lo: 2; z = z_hi * 2 + z_lo), core: 2. Of those that a mesh axis runs over, the one named last changes fastest.
Arguments:
- hidden: bfloat16 [8192, 8192], P(('rep', 'tp')), may hold values from -6 to 6
- norm_gain: bfloat16 [8192], replicated, may hold values from 0.099609375 to 1.8984375
- q_weight: bfloat16 [8192, 8192], P('rep', 'tp')
- kv_weight: bfloat16 [8192, 2048], P('rep'), may hold values from -0.0625 to 0.0625
- out_weight: bfloat16 [8192, 8192], P('tp', 'rep'), may hold values from -0.0625 to 0.0625
- held_slice: int32 [16], replicated, may hold values from 0 to 15, each once
Outputs:
- attended: bfloat16 [8192, 8192], P(('rep', 'tp'))
Inputs may be any that keep to these rules, and one draw needn't show every extreme that they name: `held_slice`: each slice number appears once.
All inputs are finite; a program needn't handle non-finite values.
Results may differ from a plain program's by a relative error of at most 0.019.
The roundings to bfloat16 on the way count: a program that leaves them out, or rounds other values in their place, can miss the bound.
Values may be sent and summed in bfloat16 or wider, within the bound.
A program may use at most 128 MiB of HBM per device.

v0:
```python
import jax
import jax.numpy as jnp
from jax import lax
from jax.sharding import PartitionSpec as P

HD = 128
HQ = 64
KVH = 8
rope_theta = 500000.0


def side_by_side(arrays, axis, dim, along):
    both = jnp.concatenate(arrays, axis=along)
    result, at, done = (lax.all_gather(both, axis, axis=dim, tiled=True), 0, [])
    for a in arrays:
        done.append(lax.slice_in_dim(result, at, at + a.shape[along], axis=along))
        at += a.shape[along]
    return tuple(done)


def rotate(states, positions):
    half = states.shape[-1] // 2
    freqs = rope_theta ** (-(jnp.arange(half, dtype=jnp.float32) * 2.0) / states.shape[-1])
    angles = positions[:, None] * freqs[None, :]
    cosine = jnp.cos(angles)[:, None, :]
    sine = jnp.sin(angles)[:, None, :]
    first = states[..., :half]
    second = states[..., half:]
    return jnp.concatenate(
        [first * cosine - second * sine, second * cosine + first * sine], axis=-1
    )


def attend(queries, keys, values):
    row_count = queries.shape[0]
    kv_local = keys.shape[1]
    per_group = queries.shape[1] // kv_local
    head_size = queries.shape[-1]
    positions = jnp.arange(row_count, dtype=jnp.int32)
    scale = 1.0 / head_size**0.5
    grouped = queries.reshape(row_count, kv_local, per_group, head_size)
    scores = jnp.einsum("sgqd,tgd->gqst", grouped, keys, preferred_element_type=jnp.float32) * scale
    allowed = positions[:, None] >= positions[None, :]
    scores = jnp.where(allowed[None, None, :, :], scores, -1e30)
    peak = jnp.max(scores, axis=-1, keepdims=True)
    weights = jnp.exp(scores - peak)
    probs = (weights / jnp.sum(weights, axis=-1, keepdims=True)).astype(jnp.bfloat16)
    context = jnp.einsum("gqst,tgd->sgqd", probs, values, preferred_element_type=jnp.float32)
    return context.astype(jnp.bfloat16).reshape(row_count, -1)


def per_device(hidden, norm_gain, q_weight, kv_weight, out_weight, held_slice):
    states = hidden.astype(jnp.float32)
    meansq = jnp.mean(states * states, axis=-1, keepdims=True)
    normed = (states * lax.rsqrt(meansq + 1e-05) * norm_gain.astype(jnp.float32)).astype(
        jnp.bfloat16
    )
    gathered = lax.all_gather(normed, "tp", axis=0, tiled=True)
    row_count = gathered.shape[0]
    width = gathered.shape[1]
    part_count = lax.axis_size("rep")
    slice_rows = width // part_count
    query_cols = q_weight.shape[1]
    heads_here = query_cols // HD
    group_size = HQ // KVH
    kv_local = max(1, heads_here // group_size)
    first_shared = lax.axis_index("tp") * heads_here // group_size
    key_cols = lax.dynamic_slice_in_dim(kv_weight, first_shared * HD, kv_local * HD, 1)
    value_cols = lax.dynamic_slice_in_dim(kv_weight, KVH * HD + first_shared * HD, kv_local * HD, 1)
    pair_cols = jnp.concatenate([key_cols, value_cols], axis=1)
    inverse = (
        jnp.zeros((part_count,), jnp.int32)
        .at[held_slice]
        .set(jnp.arange(part_count, dtype=jnp.int32))
    )
    blocks = gathered.reshape(row_count, part_count, slice_rows)
    pieces = side_by_side((q_weight, pair_cols), "rep", 0, 1)
    taken = pieces[0].shape[0] // slice_rows
    chosen = jnp.take(blocks, held_slice, axis=1).reshape(row_count, taken * slice_rows)
    queries = jnp.dot(chosen, pieces[0], preferred_element_type=jnp.float32)
    pairs = jnp.dot(chosen, pieces[1], preferred_element_type=jnp.float32)
    out_all = lax.all_gather(out_weight, "rep", axis=1, tiled=True)
    out_ordered = jnp.take(
        out_all.reshape(query_cols, part_count, slice_rows), inverse, axis=1
    ).reshape(query_cols, width)
    where_at = jnp.arange(row_count, dtype=jnp.float32)
    queries = rotate(queries.reshape(row_count, heads_here, HD), where_at).astype(jnp.bfloat16)
    keys = rotate(pairs[:, : kv_local * HD].reshape(row_count, kv_local, HD), where_at).astype(
        jnp.bfloat16
    )
    values = pairs[:, kv_local * HD :].reshape(row_count, kv_local, HD).astype(jnp.bfloat16)
    context = attend(queries, keys, values)
    partial_value = jnp.dot(context, out_ordered, preferred_element_type=jnp.float32)
    summed = lax.psum_scatter(
        partial_value.astype(jnp.bfloat16), "tp", scatter_dimension=0, tiled=True
    )
    return summed


def solution(mesh):
    return jax.shard_map(
        per_device,
        mesh=mesh,
        in_specs=(P(("rep", "tp"), None), P(), P("rep", "tp"), P("rep", None), P("tp", "rep"), P()),
        out_specs=P(("rep", "tp"), None),
        check_vma=False,
    )
```

profile of v0, /device:TPU:2, one launch (start us, length us, event | category | flops | bytes accessed | tf_op | source)
XLA Modules:
  0.0 501.7 jit_solution(620382676256943983)
XLA Ops:
  6.5 0.0 all-gather.4.cloned.1.call-start
  6.5 1.2 fusion.10
  7.8 0.7 convert_element_type.34
  8.5 2.0 fusion.12
  10.5 0.0 all-gather.4.cloned.1.call-update
  10.6 0.0 all-gather.8.cloned.1.call-start
  10.6 2.1 copy.34
  12.7 0.0 all-gather.8.cloned.1.call-update
  12.7 0.0 all-gather.6.cloned.1.call-start
  12.8 1.0 constant_dynamic-slice_fusion.1
  13.8 2.0 pad_maximum_fusion
  15.8 0.0 all-gather.6.cloned.1.call-update
  15.8 0.0 reduce-scatter.2.cloned.1.call-start
  15.9 0.7 compare_select_fusion.1
  16.5 0.6 scatter_custom_fusion
  17.2 0.1 iota_compare_fusion
  17.3 0.7 compare_and_fusion
  18.0 0.5 fusion.22
  18.5 49.8 %all-gather.4.cloned.1.call-done = bf16[512,8192]{1,0:T(8,128)(2,1)} async-done(((bf16[32,8192]{1,0:T(8,128)(2,1)}), bf16[512,8192]{1,0:T(8,128)(2,1)}) %all-gather.4.cloned.1.call-update) | async-done | bytes 8388624 | tf_op jit(solution)/shard_map/all_gather | solution.py:58
  68.3 12.0 %copy.26 = bf16[512,8192]{0,1:T(8,128)(2,1)} copy(bf16[512,8192]{1,0:T(8,128)(2,1)} %all-gather.4.cloned.1.call-done) | data formatting | bytes 16777216 | tf_op jit(solution)/shard_map/all_gather | solution.py:58
  80.3 12.2 %copy.27 = bf16[512,16,512]{2,0,1:T(8,128)(2,1)} copy(bf16[512,16,512]{0,2,1:T(8,128)(2,1)} %bitcast.58) | data formatting | bytes 16777216 | tf_op jit(solution)/shard_map/reshape | solution.py:76
  92.5 8.5 %gather_fusion = bf16[16,512,512]{2,1,0:T(8,128)(2,1)} fusion(bf16[512,16,512]{2,0,1:T(8,128)(2,1)} %copy.27, s32[1024]{0:T(1024)S(1)} %pad_clamp_fusion.1), kind=kCustom, calls=%fused_computation.clone | custom fusion | bytes 16777280 | tf_op jit(solution)/shard_map/jit(_take)/gather | solution.py:79
  100.9 7.6 %select_bitcast_fusion.1 = bf16[512,16,512]{2,0,1:T(8,128)(2,1)} fusion(bf16[16,512,512]{2,1,0:T(8,128)(2,1)} %gather_fusion, pred[16]{0:T(512)(128)(4,1)S(1)} %get-tuple-element.17), kind=kLoop, calls=%fused_computation.6 | loop fusion | flops 4194304 | bytes 16777232 | tf_op jit(solution)/shard_map/jit(_take)/select_n | solution.py:79
  108.6 12.3 %copy.28 = bf16[512,16,512]{0,2,1:T(8,128)(2,1)} copy(bf16[512,16,512]{2,0,1:T(8,128)(2,1)} %select_bitcast_fusion.1) | data formatting | bytes 16777216 | tf_op jit(solution)/shard_map/jit(_take)/select_n | solution.py:79
  120.9 59.8 %all-gather.8.cloned.1.call-done = bf16[512,8192]{0,1:T(8,128)(2,1)} async-done(((bf16[512,512]{0,1:T(8,128)(2,1)}), bf16[512,8192]{0,1:T(8,128)(2,1)}) %all-gather.8.cloned.1.call-update) | async-done | bytes 8388624 | tf_op jit(solution)/shard_map/all_gather | solution.py:82
  180.7 12.3 %copy.35 = bf16[512,16,512]{2,0,1:T(8,128)(2,1)} copy(bf16[512,16,512]{0,2,1:T(8,128)(2,1)} %bitcast.59) | data formatting | bytes 16777216 | tf_op jit(solution)/shard_map/reshape | solution.py:84
  193.0 8.1 %gather_fusion.1 = bf16[16,512,512]{2,1,0:T(8,128)(2,1)} fusion(bf16[512,16,512]{2,0,1:T(8,128)(2,1)} %copy.35, s32[1024]{0:T(1024)S(1)} %pad_clamp_fusion), kind=kCustom, calls=%fused_computation.1.clone | custom fusion | bytes 16777280 | tf_op jit(solution)/shard_map/jit(_take)/gather | solution.py:83
  201.1 8.2 %select_bitcast_fusion = bf16[512,16,512]{2,0,1:T(8,128)(2,1)} fusion(bf16[16,512,512]{2,1,0:T(8,128)(2,1)} %gather_fusion.1, pred[16]{0:T(512)(128)(4,1)S(1)} %get-tuple-element.16), kind=kLoop, calls=%fused_computation.5 | loop fusion | flops 4194304 | bytes 16777232 | tf_op jit(solution)/shard_map/jit(_take)/select_n | solution.py:83
  209.3 12.3 %copy.36 = bf16[512,16,512]{0,2,1:T(8,128)(2,1)} copy(bf16[512,16,512]{2,0,1:T(8,128)(2,1)} %select_bitcast_fusion) | data formatting | bytes 16777216 | tf_op jit(solution)/shard_map/jit(_take)/select_n | solution.py:83
  221.6 116.4 %all-gather.6.cloned.1.call-done = bf16[8192,768]{1,0:T(8,128)(2,1)} async-done(((bf16[512,768]{1,0:T(8,128)(2,1)}), bf16[8192,768]{1,0:T(8,128)(2,1)}) %all-gather.6.cloned.1.call-update) | async-done | bytes 12582928 | tf_op jit(solution)/shard_map/all_gather | solution.py:14
  338.0 7.1 %slice_bitcast_fusion = bf16[512,8192]{0,1:T(8,128)(2,1)} fusion(bf16[8192,768]{1,0:T(8,128)(2,1)} %all-gather.6.cloned.1.call-done), kind=kLoop, calls=%fused_computation.4 | loop fusion | bytes 16777216 | tf_op jit(solution)/shard_map/dot_general | solution.py:80
  345.1 11.4 %copy.29 = bf16[512,8192]{1,0:T(8,128)(2,1)} copy(bf16[512,8192]{0,1:T(8,128)(2,1)} %slice_bitcast_fusion) | data formatting | bytes 16777216 | tf_op jit(solution)/shard_map/dot_general | solution.py:80
  356.6 0.0 copy-start
  356.6 7.1 %fusion = f32[512,256]{0,1:T(8,128)S(1)} fusion(bf16[512,8192]{0,1:T(8,128)(2,1)} %bitcast.61, bf16[8192,768]{1,0:T(8,128)(2,1)} %all-gather.6.cloned.1.call-done), kind=kOutput, calls=%fused_computation.7 | convolution fusion | flops 2147483648 | bytes 13107200 | tf_op jit(solution)/shard_map/dot_general | solution.py:81
  363.7 0.6 fusion.25
  364.2 0.0 copy-done
  364.3 7.3 %fusion.32 = f32[512,4,128]{0,2,1:T(8,128)S(1)} fusion(bf16[512,8192,1]{0,1,2:T(8,128)(2,1)} %bitcast.62, bf16[4,128,8192]{2,1,0:T(8,128)(2,1)S(1)} %bitcast.63), kind=kOutput, calls=%fused_computation.62 | convolution fusion | flops 4294967296 | bytes 17825792 | tf_op jit(solution)/shard_map/dot_general | solution.py:80
  371.5 0.2 subtract_convert_fusion
  371.7 0.9 fusion.3
  372.6 0.9 fusion.2
  373.6 1.5 fusion.7
  375.1 10.2 %convolution_convert_fusion = bf16[512,8192]{1,0:T(8,128)(2,1)} fusion(bf16[512,512]{0,1:T(8,128)(2,1)S(1)} %bitcast.64, bf16[512,8192]{0,1:T(8,128)(2,1)} %bitcast.60), kind=kOutput, calls=%fused_computation.3 | convolution fusion | flops 4299161600 | bytes 17301504 | tf_op jit(solution)/shard_map/dot_general | solution.py:93
  385.3 0.0 reduce-scatter.2.cloned.1.call-update
  385.3 109.8 %reduce-scatter.2.cloned.1.call-done = bf16[32,8192]{1,0:T(8,128)(2,1)} async-done(((bf16[512,8192]{1,0:T(8,128)(2,1)}), bf16[32,8192]{1,0:T(8,128)(2,1)}) %reduce-scatter.2.cloned.1.call-update) | async-done | bytes 524304 | tf_op jit(solution)/shard_map/reduce_scatter | solution.py:94
  (7 shorter events, 0.1 us)
Async XLA Ops:
  6.5 61.8 %all-gather.4.cloned.1.call-start = ((), (), s32[]{:S(2)}) async-start(), calls=%async_computation.1 | async-start | bytes 8912896 | tf_op jit(solution)/shard_map/all_gather | solution.py:58
  10.6 170.1 %all-gather.8.cloned.1.call-start = ((), (), s32[]{:S(2)}) async-start(), calls=%async_computation.3 | async-start | bytes 8912896 | tf_op jit(solution)/shard_map/all_gather | solution.py:82
  12.7 325.3 %all-gather.6.cloned.1.call-start = ((), (), s32[]{:S(2)}) async-start(), calls=%async_computation.2 | async-start | bytes 13369344 | tf_op jit(solution)/shard_map/all_gather | solution.py:14
  15.8 479.4 %reduce-scatter.2.cloned.1.call-start = ((), (), s32[]{:S(2)}) async-start(), calls=%async_computation.4 | async-start | bytes 8912896 | tf_op jit(solution)/shard_map/reduce_scatter | solution.py:94
  356.6 7.7 %copy-start = (bf16[512,8192]{1,0:T(8,128)(2,1)S(1)}, bf16[512,8192]{1,0:T(8,128)(2,1)}, u32[]{:S(2)}) copy-start(bf16[512,8192]{1,0:T(8,128)(2,1)} %copy.29) | copy-start | bytes 25165828
Sparse Core Ops, SparseCore 0:
  10.7 57.5 all-gather.3
  70.8 109.8 all-gather.7
  183.2 154.7 all-gather.5
  385.4 109.6 reduce-scatter.1
where the time goes:
time: 504 us; the launch traced here: 502 us
  waiting for transfers between devices  336 us (67%)
  local copies, waits for them, and re-layouts  99.9 us (20%)
  matrix products  27 us (5%)
  other arithmetic  25.4 us (5%)
  between operations  13.3 us (3%)
    all_gather x1, waiting for transfers between devices, side_by_side(): result, at, done = (lax.all_gather(both, axis, axis=dim, tiled=True), 0, [])  116 us
    reduce_scatter x1, waiting for transfers between devices, per_device(): lax.psum_scatter(partial_value.astype(jnp.bfloat16), 'tp', scatter_dimens...  110 us
    all_gather x1, waiting for transfers between devices, per_device(): out_all = lax.all_gather(out_weight, 'rep', axis=1, tiled=True)  59.8 us
    all_gather x1, waiting for transfers between devices, per_device(): gathered = lax.all_gather(normed, 'tp', axis=0, tiled=True)  49.8 us
    dot_general x2, local copies, waits for them, and re-layouts, per_device(): queries = jnp.dot(chosen, pieces[0], preferred_element_type=jnp.float32)  18.6 us
    select_n x1, local copies, waits for them, and re-layouts, per_device(): jnp.take(out_all.reshape(query_cols, part_count, slice_rows), inverse, ax...  12.3 us
    select_n x1, local copies, waits for them, and re-layouts, per_device(): jnp.take(blocks, held_slice, axis=1).reshape(row_count, taken * slice_rows)  12.3 us
    reshape x1, local copies, waits for them, and re-layouts, per_device(): out_all.reshape(query_cols, part_count, slice_rows)  12.3 us
  transfers between devices with their start and end apart: 4, of which 4 were waited for; matrix products, arithmetic and copies ran while one was open for 20% of the time, Pallas kernels for 0%

commit v1 on v0

--- a/solution.py
+++ b/solution.py
@@ -79,7 +79,8 @@
     chosen = jnp.take(blocks, held_slice, axis=1).reshape(row_count, taken * slice_rows)
     queries = jnp.dot(chosen, pieces[0], preferred_element_type=jnp.float32)
     pairs = jnp.dot(chosen, pieces[1], preferred_element_type=jnp.float32)
-    out_all = lax.all_gather(out_weight, "rep", axis=1, tiled=True)
+    sent = jnp.stack([out_weight] * lax.axis_size("rep"))
+    out_all = jnp.concatenate(lax.all_to_all(sent, "rep", 0, 0), axis=1)
     out_ordered = jnp.take(
         out_all.reshape(query_cols, part_count, slice_rows), inverse, axis=1
     ).reshape(query_cols, width)

time: 504 us -> 545 us (1.081)
  waiting for transfers between devices: 336 us -> 378 us
  starting transfers between devices: 0.13 us -> 11.7 us
  local copies, waits for them, and re-layouts: 99.9 us -> 90.1 us
    all_gather x1, waiting for transfers between devices: 49.8 us -> 150 us  [per_device(): gathered = lax.all_gather(normed, 'tp', axis=0, tiled=True)]
    all_gather x1 -> x0, waiting for transfers between devices: 59.8 us -> none  [per_device(): out_all = lax.all_gather(out_weight, 'rep', axis=1, tiled=True)]
    all_gather x1, waiting for transfers between devices: 116 us -> 78.7 us  [side_by_side(): result, at, done = (lax.all_gather(both, axis, axis=dim, tiled=True), 0, [])]
    all_to_all x0 -> x1, waiting for transfers between devices: none -> 34.9 us  [per_device(): out_all = jnp.concatenate(lax.all_to_all(sent, 'rep', 0, 0), axis=1)]
    reshape x1 -> x0, local copies, waits for them, and re-layouts: 12.3 us -> none  [per_device(): out_all.reshape(query_cols, part_count, slice_rows)]
    all_to_all x0 -> x1, starting transfers between devices: none -> 11.6 us  [per_device(): out_all = jnp.concatenate(lax.all_to_all(sent, 'rep', 0, 0), axis=1)]
  transfers between devices with their start and end apart: 4 -> 4, of which waited for: 4 -> 4; matrix products, arithmetic and copies ran while one was open for 20% -> 16% of each run, Pallas kernels for 0% -> 0%
where the time goes in v1:
time: 545 us; the launch traced here: 543 us
  waiting for transfers between devices  378 us (69%)
  local copies, waits for them, and re-layouts  90.1 us (17%)
  matrix products  27 us (5%)
  other arithmetic  23.4 us (4%)
  between operations  13.3 us (2%)
  starting transfers between devices  11.7 us (2%)
    all_gather x1, waiting for transfers between devices, per_device(): gathered = lax.all_gather(normed, 'tp', axis=0, tiled=True)  150 us
    reduce_scatter x1, waiting for transfers between devices, per_device(): lax.psum_scatter(partial_value.astype(jnp.bfloat16), 'tp', scatter_dimens...  114 us
    all_gather x1, waiting for transfers between devices, side_by_side(): result, at, done = (lax.all_gather(both, axis, axis=dim, tiled=True), 0, [])  78.7 us
    all_to_all x1, waiting for transfers between devices, per_device(): out_all = jnp.concatenate(lax.all_to_all(sent, 'rep', 0, 0), axis=1)  34.9 us
    dot_general x2, local copies, waits for them, and re-layouts, per_device(): queries = jnp.dot(chosen, pieces[0], preferred_element_type=jnp.float32)  18.6 us
    reshape x1, local copies, waits for them, and re-layouts, per_device(): blocks = gathered.reshape(row_count, part_count, slice_rows)  12.3 us
    select_n x1, local copies, waits for them, and re-layouts, per_device(): jnp.take(blocks, held_slice, axis=1).reshape(row_count, taken * slice_rows)  12.3 us
    all_gather x1, local copies, waits for them, and re-layouts, per_device(): gathered = lax.all_gather(normed, 'tp', axis=0, tiled=True)  11.9 us
  transfers between devices with their start and end apart: 4, of which 4 were waited for; matrix products, arithmetic and copies ran while one was open for 16% of the time, Pallas kernels for 0%

profile of v1, /device:TPU:2, one launch (start us, length us, event | category | flops | bytes accessed | tf_op | source)
XLA Modules:
  0.0 543.0 jit_solution(5847224088328502347)
XLA Ops:
  6.5 0.0 all-gather.3.cloned.1.call-start
  6.5 1.2 fusion.10
  7.8 0.7 convert_element_type.34
  8.5 2.0 fusion.12
  10.5 0.0 all-gather.3.cloned.1.call-update
  10.6 0.0 all-gather.5.cloned.1.call-start
  10.6 1.0 constant_dynamic-slice_fusion.1
  11.6 2.0 pad_maximum_fusion
  13.6 0.0 all-gather.5.cloned.1.call-update
  13.7 5.2 stack.2
  18.9 0.0 copy-start.1
  18.9 11.6 %all-to-all-start = ((bf16[16,512,512]{2,1,0:T(8,128)(2,1)}), bf16[16,512,512]{2,1,0:T(8,128)(2,1)}, u32[]{:S(2)}, u32[]{:S(2)}) async-start(bf16[16,512,512]{2,1,0:T(8,128)(2,1)} %stack.2), calls=%async_computation | async-start | bytes 16777216 | tf_op jit(solution)/shard_map/all_to_all | solution.py:83
  30.5 0.0 reduce-scatter.2.cloned.1.call-start
  30.5 0.0 copy-done.1
  30.5 0.6 scatter_custom_fusion
  31.2 0.1 iota_compare_fusion
  31.3 0.5 fusion.22
  31.9 149.6 %all-gather.3.cloned.1.call-done = bf16[512,8192]{1,0:T(8,128)(2,1)} async-done(((bf16[32,8192]{1,0:T(8,128)(2,1)}), bf16[512,8192]{1,0:T(8,128)(2,1)}) %all-gather.3.cloned.1.call-update) | async-done | bytes 8388624 | tf_op jit(solution)/shard_map/all_gather | solution.py:58
  181.5 11.9 %copy.24 = bf16[512,8192]{0,1:T(8,128)(2,1)} copy(bf16[512,8192]{1,0:T(8,128)(2,1)} %all-gather.3.cloned.1.call-done) | data formatting | bytes 16777216 | tf_op jit(solution)/shard_map/all_gather | solution.py:58
  193.4 12.3 %copy.25 = bf16[512,16,512]{2,0,1:T(8,128)(2,1)} copy(bf16[512,16,512]{0,2,1:T(8,128)(2,1)} %bitcast.58) | data formatting | bytes 16777216 | tf_op jit(solution)/shard_map/reshape | solution.py:76
  205.7 8.2 %gather_fusion = bf16[16,512,512]{2,1,0:T(8,128)(2,1)} fusion(bf16[512,16,512]{2,0,1:T(8,128)(2,1)} %copy.25, s32[1024]{0:T(1024)S(1)} %pad_clamp_fusion.1), kind=kCustom, calls=%fused_computation.clone | custom fusion | bytes 16777280 | tf_op jit(solution)/shard_map/jit(_take)/gather | solution.py:79
  213.9 7.5 %select_bitcast_fusion.1 = bf16[512,16,512]{2,0,1:T(8,128)(2,1)} fusion(bf16[16,512,512]{2,1,0:T(8,128)(2,1)} %gather_fusion, pred[16]{0:T(512)(128)(4,1)S(1)} %compare_and_fusion.1), kind=kLoop, calls=%fused_computation.6 | loop fusion | flops 4194304 | bytes 16777232 | tf_op jit(solution)/shard_map/jit(_take)/select_n | solution.py:79
  221.3 12.3 %copy.26 = bf16[512,16,512]{0,2,1:T(8,128)(2,1)} copy(bf16[512,16,512]{2,0,1:T(8,128)(2,1)} %select_bitcast_fusion.1) | data formatting | bytes 16777216 | tf_op jit(solution)/shard_map/jit(_take)/select_n | solution.py:79
  233.6 34.9 %all-to-all-done = bf16[16,512,512]{2,1,0:T(8,128)(2,1)} async-done(((bf16[16,512,512]{2,1,0:T(8,128)(2,1)}), bf16[16,512,512]{2,1,0:T(8,128)(2,1)}, u32[]{:S(2)}, u32[]{:S(2)}) %all-to-all-start) | async-done | bytes 8388640 | tf_op jit(solution)/shard_map/all_to_all | solution.py:83
  268.5 8.3 %gather_fusion.1 = bf16[16,512,512]{2,1,0:T(8,128)(2,1)} fusion(bf16[512,16,512]{2,0,1:T(8,128)(2,1)} %bitcast.17, s32[1024]{0:T(1024)S(1)} %pad_clamp_fusion), kind=kCustom, calls=%fused_computation.1.clone | custom fusion | bytes 16777280 | tf_op jit(solution)/shard_map/jit(_take)/gather | solution.py:84
  276.8 7.6 %select_bitcast_fusion = bf16[512,16,512]{2,0,1:T(8,128)(2,1)} fusion(bf16[16,512,512]{2,1,0:T(8,128)(2,1)} %gather_fusion.1, pred[16]{0:T(512)(128)(4,1)S(1)} %compare_and_fusion), kind=kLoop, calls=%fused_computation.5 | loop fusion | flops 4194304 | bytes 16777232 | tf_op jit(solution)/shard_map/jit(_take)/select_n | solution.py:84
  284.4 11.8 %copy.32 = bf16[512,16,512]{0,2,1:T(8,128)(2,1)} copy(bf16[512,16,512]{2,0,1:T(8,128)(2,1)} %select_bitcast_fusion) | data formatting | bytes 16777216 | tf_op jit(solution)/shard_map/jit(_take)/select_n | solution.py:84
  296.1 78.7 %all-gather.5.cloned.1.call-done = bf16[8192,768]{1,0:T(8,128)(2,1)} async-done(((bf16[512,768]{1,0:T(8,128)(2,1)}), bf16[8192,768]{1,0:T(8,128)(2,1)}) %all-gather.5.cloned.1.call-update) | async-done | bytes 12582928 | tf_op jit(solution)/shard_map/all_gather | solution.py:14
  374.8 7.2 %slice_bitcast_fusion = bf16[512,8192]{0,1:T(8,128)(2,1)} fusion(bf16[8192,768]{1,0:T(8,128)(2,1)} %all-gather.5.cloned.1.call-done), kind=kLoop, calls=%fused_computation.4 | loop fusion | bytes 16777216 | tf_op jit(solution)/shard_map/dot_general | solution.py:80
  382.1 11.3 %copy.27 = bf16[512,8192]{1,0:T(8,128)(2,1)} copy(bf16[512,8192]{0,1:T(8,128)(2,1)} %slice_bitcast_fusion) | data formatting | bytes 16777216 | tf_op jit(solution)/shard_map/dot_general | solution.py:80
  393.4 0.0 copy-start
  393.4 7.1 %fusion = f32[512,256]{0,1:T(8,128)S(1)} fusion(bf16[512,8192]{0,1:T(8,128)(2,1)} %bitcast.60, bf16[8192,768]{1,0:T(8,128)(2,1)} %all-gather.5.cloned.1.call-done), kind=kOutput, calls=%fused_computation.7 | convolution fusion | flops 2147483648 | bytes 13107200 | tf_op jit(solution)/shard_map/dot_general | solution.py:81
  400.5 0.6 fusion.25
  401.1 0.0 copy-done
  401.1 7.3 %fusion.32 = f32[512,4,128]{0,2,1:T(8,128)S(1)} fusion(bf16[512,8192,1]{0,1,2:T(8,128)(2,1)} %bitcast.61, bf16[4,128,8192]{2,1,0:T(8,128)(2,1)S(1)} %bitcast.62), kind=kOutput, calls=%fused_computation.62 | convolution fusion | flops 4294967296 | bytes 17825792 | tf_op jit(solution)/shard_map/dot_general | solution.py:80
  408.4 0.2 subtract_convert_fusion
  408.6 0.9 fusion.3
  409.5 0.9 fusion.2
  410.4 1.5 fusion.7
  411.9 10.2 %convolution_convert_fusion = bf16[512,8192]{1,0:T(8,128)(2,1)} fusion(bf16[512,512]{0,1:T(8,128)(2,1)S(1)} %bitcast.63, bf16[512,8192]{0,1:T(8,128)(2,1)} %bitcast.59), kind=kOutput, calls=%fused_computation.3 | convolution fusion | flops 4299161600 | bytes 17301504 | tf_op jit(solution)/shard_map/dot_general | solution.py:94
  422.1 0.0 reduce-scatter.2.cloned.1.call-update
  422.1 114.3 %reduce-scatter.2.cloned.1.call-done = bf16[32,8192]{1,0:T(8,128)(2,1)} async-done(((bf16[512,8192]{1,0:T(8,128)(2,1)}), bf16[32,8192]{1,0:T(8,128)(2,1)}) %reduce-scatter.2.cloned.1.call-update) | async-done | bytes 524304 | tf_op jit(solution)/shard_map/reduce_scatter | solution.py:95
  (10 shorter events, 0.1 us)
Async XLA Ops:
  6.5 175.0 %all-gather.3.cloned.1.call-start = ((), (), s32[]{:S(2)}) async-start(), calls=%async_computation.2 | async-start | bytes 8912896 | tf_op jit(solution)/shard_map/all_gather | solution.py:58
  10.6 364.2 %all-gather.5.cloned.1.call-start = ((), (), s32[]{:S(2)}) async-start(), calls=%async_computation.3 | async-start | bytes 13369344 | tf_op jit(solution)/shard_map/all_gather | solution.py:14
  18.9 11.7 %copy-start.1 = (s32[16]{0:T(128)S(1)}, s32[16]{0:T(128)}, u32[]{:S(2)}) copy-start(s32[16]{0:T(128)} %param.13) | copy-start | bytes 196
  18.9 249.6 %all-to-all-start = ((bf16[16,512,512]{2,1,0:T(8,128)(2,1)}), bf16[16,512,512]{2,1,0:T(8,128)(2,1)}, u32[]{:S(2)}, u32[]{:S(2)}) async-start(bf16[16,512,512]{2,1,0:T(8,128)(2,1)} %stack.2), calls=%async_computation | async-start | bytes 16777216 | tf_op jit(solution)/shard_map/all_to_all | solution.py:83
  30.5 506.0 %reduce-scatter.2.cloned.1.call-start = ((), (), s32[]{:S(2)}) async-start(), calls=%async_computation.4 | async-start | bytes 8912896 | tf_op jit(solution)/shard_map/reduce_scatter | solution.py:95
  393.4 7.7 %copy-start = (bf16[512,8192]{1,0:T(8,128)(2,1)S(1)}, bf16[512,8192]{1,0:T(8,128)(2,1)}, u32[]{:S(2)}) copy-start(bf16[512,8192]{1,0:T(8,128)(2,1)} %copy.27) | copy-start | bytes 25165828
Sparse Core Ops, SparseCore 0:
  10.7 170.7 all-gather.2
  184.0 190.7 all-gather.4
  422.3 114.1 reduce-scatter.1
